TPU v7x, 128 devices: a whole 4x4x4 slice. The times are simulated.
128 devices in a mesh: section: 8 (over y, core), seq: 16 (over z, x).
Axes of the slice: x: 4, y: 4, z: 4, core: 2. Of those that a mesh axis runs over, the one named last changes fastest.
Arguments:
- queries: bfloat16 [8, 2, 2048, 4096], P('section', None, 'seq'), may hold values from -20 to 20
- keys_values: bfloat16 [8, 2, 2048, 8, 256], P('section', None, 'seq'), may hold values from -20 to 20
- lengths: int32 [8, 2, 4], P('section'), may hold values from 1 to 1024, 2048 in all within a row
- order: int32 [8, 2], P('section'), may hold values from 0 to 1, each once within a row
Outputs:
- handoff: bfloat16 [8, 2, 2048, 4096], P('section', None, 'seq')
Inputs may be any that keep to these rules, and one draw needn't show every extreme that they name: Each row holds the lengths of 4 documents packed end to end, summing to 2048, the longest exactly 1024. `order`: each row is a permutation of the microbatch numbers.
All inputs are finite; a program needn't handle non-finite values.
Results may differ from a plain program's by a relative error of at most 0.0037.
Values may be sent and summed in bfloat16 or wider, within the bound.
No kernel may reach another device: no remote copies, remote signals or barrier semaphores. Data moves between devices by JAX's collectives and lax.ppermute only.
A program may use at most 64 MiB of HBM per device.

v0:
```python
import jax
import jax.numpy as jnp
from jax import lax
from jax.sharding import PartitionSpec as P

HD = 128
QH = 32
KVH = 8


def shortened(value):
    return jax.tree.map(lambda a: a.astype(jnp.bfloat16) if a.dtype == jnp.float32 else a, value)


def passed_along(block, axis, distance):
    devices = range(lax.axis_size(axis))
    route = [((i - distance) % len(devices), i) for i in devices]
    return lax.ppermute(block, axis, route)


def segment_ids(lengths_row, rows_all):
    ends = jnp.cumsum(lengths_row)
    position = jnp.arange(rows_all, dtype=jnp.int32)
    return jnp.sum((position[:, None] >= ends[None, :]).astype(jnp.int32), axis=1)


def attend(query_rows, pair_rows, lengths_row):
    rows_all = query_rows.shape[0]
    head_count = query_rows.shape[1] // HD
    pair_count = pair_rows.shape[1] // (2 * HD)
    share_count = head_count // pair_count
    scaling = HD ** (-0.5)
    segment = segment_ids(lengths_row, rows_all)
    position = jnp.arange(rows_all, dtype=jnp.int32)
    block_rows = min(512, rows_all)

    def one_block(block_index):
        row_start = block_index * block_rows
        query_block = lax.dynamic_slice_in_dim(query_rows, row_start, block_rows, 0)
        segment_query = lax.dynamic_slice_in_dim(segment, row_start, block_rows, 0)
        position_query = lax.dynamic_slice_in_dim(position, row_start, block_rows, 0)
        allowed = (segment_query[:, None] == segment[None, :]) & (
            position[None, :] <= position_query[:, None]
        )
        results = []
        for head_index in range(head_count):
            pair_head = head_index // share_count
            query_cols = query_block[:, head_index * HD : (head_index + 1) * HD]
            key_cols = pair_rows[:, pair_head * 2 * HD : pair_head * 2 * HD + HD]
            value_cols = pair_rows[:, pair_head * 2 * HD + HD : (pair_head + 1) * 2 * HD]
            scores = (
                lax.dot_general(
                    query_cols,
                    key_cols,
                    (((1,), (1,)), ((), ())),
                    preferred_element_type=jnp.float32,
                )
                * scaling
            )
            peaks = jnp.max(jnp.where(allowed, scores, -jnp.inf), axis=1, keepdims=True)
            weights = jnp.where(allowed, jnp.exp(scores - peaks), jnp.float32(0.0))
            totals = jnp.sum(weights, axis=1, keepdims=True)
            mixed = (
                jnp.dot(
                    weights.astype(jnp.bfloat16), value_cols, preferred_element_type=jnp.float32
                )
                / totals
            )
            results.append(mixed.astype(jnp.bfloat16))
        return jnp.concatenate(results, axis=1)

    blocks = lax.map(one_block, jnp.arange(rows_all // block_rows, dtype=jnp.int32))
    return blocks.reshape(rows_all, head_count * HD)


def reorder(stacked, order_row):
    picked_all = []
    for slot in range(stacked.shape[0]):
        picked = stacked[0]
        picked = jnp.where(order_row[slot] == 1, stacked[1], picked)
        picked_all.append(picked)
    return jnp.stack(picked_all, axis=0)


def local(queries, keys_values, lengths, order):
    n_seq = lax.axis_size("seq")
    micro = queries.shape[1]
    tok_rows = queries.shape[2]
    all_rows = tok_rows * n_seq
    per_device = QH // n_seq
    repeat_count = max(1, n_seq // KVH)
    kv_local = max(1, KVH // n_seq)
    query_split = queries.reshape(micro, tok_rows, n_seq, per_device * HD)
    wide = jnp.repeat(keys_values.reshape(micro, tok_rows, KVH, 2 * HD), repeat_count, axis=2)
    head_queries, head_pairs = (
        lax.all_to_all(query_split, "seq", split_axis=2, concat_axis=1, tiled=True),
        lax.all_to_all(wide, "seq", split_axis=2, concat_axis=1, tiled=True),
    )
    head_queries = head_queries.reshape(micro, all_rows, per_device * HD)
    head_pairs = head_pairs.reshape(micro, all_rows, kv_local * 2 * HD)
    contexts = jnp.stack(
        [
            attend(head_queries[index_mb], head_pairs[index_mb], lengths[0, index_mb])
            for index_mb in range(micro)
        ],
        axis=0,
    )
    contexts = contexts.reshape(micro, all_rows, 1, per_device * HD)
    back = lax.all_to_all(
        shortened(contexts), "seq", split_axis=1, concat_axis=2, tiled=True
    ).astype(contexts.dtype)
    result = passed_along(shortened(reorder(back, order[0])), "section", 1)
    return result.reshape(1, micro, tok_rows, QH * HD)


def solution(mesh):
    placed = (
        P("section", None, "seq", None),
        P("section", None, "seq", None, None),
        P("section", None, None),
        P("section", None),
    )
    return jax.shard_map(
        local,
        mesh=mesh,
        in_specs=placed,
        out_specs=P("section", None, "seq", None),
        check_vma=False,
    )
```

profile of v0, /device:TPU:0, one launch (start us, length us, event | category | flops | bytes accessed | tf_op | source)
XLA Modules:
  0.0 293.3 jit_solution(14216556808177884193)
XLA Ops:
  0.0 3.1 %copy.45 = bf16[1,2,128,4096]{2,3,1,0:T(8,128)(2,1)S(1)} copy(bf16[1,2,128,4096]{3,2,1,0:T(8,128)(2,1)} %param.8) | data formatting | bytes 4194304 | tf_op args[0]
  3.1 2.6 copy.46
  5.7 8.0 %all-to-all-start = ((bf16[2,128,16,256]{3,1,0,2:T(8,128)(2,1)}), bf16[2,128,16,256]{3,1,0,2:T(8,128)(2,1)S(1)}, u32[]{:S(2)}, u32[]{:S(2)}) async-start(bf16[2,128,16,256]{3,1,0,2:T(8,128)(2,1)} %copy.46), calls=%async_computation | async-start | bytes 4194304 | tf_op jit(solution)/shard_map/all_to_all | solution.py:96
  13.7 1.4 copy.47
  15.2 30.3 %all-to-all-done = bf16[2,128,16,256]{3,1,0,2:T(8,128)(2,1)S(1)} async-done(((bf16[2,128,16,256]{3,1,0,2:T(8,128)(2,1)}), bf16[2,128,16,256]{3,1,0,2:T(8,128)(2,1)S(1)}, u32[]{:S(2)}, u32[]{:S(2)}) %all-to-all-start) | async-done | bytes 2097184 | tf_op jit(solution)/shard_map/all_to_all | solution.py:96
  45.5 1.6 broadcast_in_dim.48
  47.1 4.4 %all-to-all-start.1 = ((bf16[2,128,16,256]{3,1,0,2:T(8,128)(2,1)}), bf16[2,128,16,256]{3,1,0,2:T(8,128)(2,1)}, u32[]{:S(2)}, u32[]{:S(2)}) async-start(bf16[2,128,16,256]{3,1,0,2:T(8,128)(2,1)} %bitcast.62), calls=%async_computation.1 | async-start | bytes 4194304 | tf_op jit(solution)/shard_map/all_to_all | solution.py:97
  52.1 1.5 fusion.69
  53.6 27.9 %all-to-all-done.1 = bf16[2,128,16,256]{3,1,0,2:T(8,128)(2,1)} async-done(((bf16[2,128,16,256]{3,1,0,2:T(8,128)(2,1)}), bf16[2,128,16,256]{3,1,0,2:T(8,128)(2,1)}, u32[]{:S(2)}, u32[]{:S(2)}) %all-to-all-start.1) | async-done | bytes 2097184 | tf_op jit(solution)/shard_map/all_to_all | solution.py:97
  81.5 2.7 fusion.68
  84.3 59.1 %while.22 = (s32[]{:T(128)}, bf16[4,512,256]{2,1,0:T(8,128)(2,1)S(1)}, s32[4]{0:T(128)S(1)}, s32[2048]{0:T(1024)S(1)}, s32[2048]{0:T(1024)S(1)}, /*index=5*/bf16...) while((s32[]{:T(128)}, ...), condition=%wide.region_7.8_spmd.clone, body=%wide.region_2.7_spmd.clone.sunk | while | flops 1113323520 | bytes 46268652 | solution.py:72
  84.3 0.7 dynamic_slice.39
  85.8 3.8 %select_reduce_fusion.6 = (f32[512]{0:T(512)S(1)}, f32[512,2048]{1,0:T(8,128)}) fusion(s32[512]{0:T(512)S(1)} %dynamic_slice.40, s32[2048]{0:T(1024)S(1)} %get-tuple-element.339, s32[2048]{0:T(1024)S(1)} %get-tuple-element.338, s32[512]{0:T(512)S(1)} %dynamic_slice.41, bf16[2048,256]{1,0:T(8,128)(2,1)S(1)} %get-tuple-element.341, ...), kind=kOutput, calls=%fused_computation.3.clone.1 | convolution fusion | flops 274726400 | bytes 4872196 | tf_op jit(solution)/shard_map/while/body/eval_jaxpr/dot_general | solution.py:52
  89.6 4.6 %fusion.91 = (f32[512]{0:T(512)S(1)}, f32[512]{0:T(512)S(1)}, f32[512,2048]{1,0:T(8,128)S(1)}) fusion(f32[512,2048]{1,0:T(8,128)} %get-tuple-element.258, f32[512]{0:T(512)S(1)} %get-tuple-element.259, s32[512]{0:T(512)S(1)} %dynamic_slice.40, s32[2048]{0:T(1024)S(1)} %get-tuple-element.339, s32[2048]{0:T(1024)S(1)} %get-tuple-element.338, ...), kind=kOutput, calls=%fused_computation.5.clone.1 | convolution fusion | flops 278920192 | bytes 9070600 | tf_op jit(solution)/shard_map/while/body/eval_jaxpr/dot_general | solution.py:52
  94.2 1.5 fusion.94
  95.6 1.7 fusion.92
  97.4 1.5 fusion.93
  99.0 0.7 dynamic_slice.39
  100.6 3.8 %select_reduce_fusion.6 = (f32[512]{0:T(512)S(1)}, f32[512,2048]{1,0:T(8,128)}) fusion(s32[512]{0:T(512)S(1)} %dynamic_slice.40, s32[2048]{0:T(1024)S(1)} %get-tuple-element.339, s32[2048]{0:T(1024)S(1)} %get-tuple-element.338, s32[512]{0:T(512)S(1)} %dynamic_slice.41, bf16[2048,256]{1,0:T(8,128)(2,1)S(1)} %get-tuple-element.341, ...), kind=kOutput, calls=%fused_computation.3.clone.1 | convolution fusion | flops 274726400 | bytes 4872196 | tf_op jit(solution)/shard_map/while/body/eval_jaxpr/dot_general | solution.py:52
  104.4 4.6 %fusion.91 = (f32[512]{0:T(512)S(1)}, f32[512]{0:T(512)S(1)}, f32[512,2048]{1,0:T(8,128)S(1)}) fusion(f32[512,2048]{1,0:T(8,128)} %get-tuple-element.258, f32[512]{0:T(512)S(1)} %get-tuple-element.259, s32[512]{0:T(512)S(1)} %dynamic_slice.40, s32[2048]{0:T(1024)S(1)} %get-tuple-element.339, s32[2048]{0:T(1024)S(1)} %get-tuple-element.338, ...), kind=kOutput, calls=%fused_computation.5.clone.1 | convolution fusion | flops 278920192 | bytes 9070600 | tf_op jit(solution)/shard_map/while/body/eval_jaxpr/dot_general | solution.py:52
  108.9 1.5 fusion.94
  110.4 1.7 fusion.92
  112.1 1.5 fusion.93
  113.8 0.7 dynamic_slice.39
  115.3 3.8 %select_reduce_fusion.6 = (f32[512]{0:T(512)S(1)}, f32[512,2048]{1,0:T(8,128)}) fusion(s32[512]{0:T(512)S(1)} %dynamic_slice.40, s32[2048]{0:T(1024)S(1)} %get-tuple-element.339, s32[2048]{0:T(1024)S(1)} %get-tuple-element.338, s32[512]{0:T(512)S(1)} %dynamic_slice.41, bf16[2048,256]{1,0:T(8,128)(2,1)S(1)} %get-tuple-element.341, ...), kind=kOutput, calls=%fused_computation.3.clone.1 | convolution fusion | flops 274726400 | bytes 4872196 | tf_op jit(solution)/shard_map/while/body/eval_jaxpr/dot_general | solution.py:52
  119.2 4.6 %fusion.91 = (f32[512]{0:T(512)S(1)}, f32[512]{0:T(512)S(1)}, f32[512,2048]{1,0:T(8,128)S(1)}) fusion(f32[512,2048]{1,0:T(8,128)} %get-tuple-element.258, f32[512]{0:T(512)S(1)} %get-tuple-element.259, s32[512]{0:T(512)S(1)} %dynamic_slice.40, s32[2048]{0:T(1024)S(1)} %get-tuple-element.339, s32[2048]{0:T(1024)S(1)} %get-tuple-element.338, ...), kind=kOutput, calls=%fused_computation.5.clone.1 | convolution fusion | flops 278920192 | bytes 9070600 | tf_op jit(solution)/shard_map/while/body/eval_jaxpr/dot_general | solution.py:52
  123.7 1.5 fusion.94
  125.2 1.7 fusion.92
  126.9 1.5 fusion.93
  128.6 0.7 dynamic_slice.39
  130.1 3.8 %select_reduce_fusion.6 = (f32[512]{0:T(512)S(1)}, f32[512,2048]{1,0:T(8,128)}) fusion(s32[512]{0:T(512)S(1)} %dynamic_slice.40, s32[2048]{0:T(1024)S(1)} %get-tuple-element.339, s32[2048]{0:T(1024)S(1)} %get-tuple-element.338, s32[512]{0:T(512)S(1)} %dynamic_slice.41, bf16[2048,256]{1,0:T(8,128)(2,1)S(1)} %get-tuple-element.341, ...), kind=kOutput, calls=%fused_computation.3.clone.1 | convolution fusion | flops 274726400 | bytes 4872196 | tf_op jit(solution)/shard_map/while/body/eval_jaxpr/dot_general | solution.py:52
  133.9 4.6 %fusion.91 = (f32[512]{0:T(512)S(1)}, f32[512]{0:T(512)S(1)}, f32[512,2048]{1,0:T(8,128)S(1)}) fusion(f32[512,2048]{1,0:T(8,128)} %get-tuple-element.258, f32[512]{0:T(512)S(1)} %get-tuple-element.259, s32[512]{0:T(512)S(1)} %dynamic_slice.40, s32[2048]{0:T(1024)S(1)} %get-tuple-element.339, s32[2048]{0:T(1024)S(1)} %get-tuple-element.338, ...), kind=kOutput, calls=%fused_computation.5.clone.1 | convolution fusion | flops 278920192 | bytes 9070600 | tf_op jit(solution)/shard_map/while/body/eval_jaxpr/dot_general | solution.py:52
  138.5 1.5 fusion.94
  140.0 1.7 fusion.92
  141.7 1.5 fusion.93
  143.5 68.4 %while.23 = (s32[]{:T(128)}, bf16[4,512,256]{2,1,0:T(8,128)(2,1)S(1)}, s32[4]{0:T(128)S(1)}, s32[2048]{0:T(1024)S(1)}, s32[2048]{0:T(1024)S(1)}, /*index=5*/bf16...) while((s32[]{:T(128)}, ...), condition=%wide.region_15.16_spmd.clone, body=%wide.region_10.15_spmd.clone.sunk | while | flops 1113323520 | bytes 46268652 | solution.py:72
  143.7 0.6 dynamic_slice.42
  145.1 4.0 %select_reduce_fusion.7 = (f32[512]{0:T(512)S(1)}, f32[512,2048]{1,0:T(8,128)}) fusion(s32[512]{0:T(512)S(1)} %dynamic_slice.43, s32[2048]{0:T(1024)S(1)} %get-tuple-element.303, s32[2048]{0:T(1024)S(1)} %get-tuple-element.302, s32[512]{0:T(512)S(1)} %dynamic_slice.44, bf16[2048,256]{1,0:T(8,128)(2,1)} %get-tuple-element.305, ...), kind=kOutput, calls=%fused_computation.33.clone.1 | convolution fusion | flops 274726400 | bytes 4872196 | tf_op jit(solution)/shard_map/while/body/eval_jaxpr/dot_general | solution.py:52
  149.1 4.7 %fusion.99 = (f32[512]{0:T(512)S(1)}, f32[512]{0:T(512)S(1)}, f32[512,2048]{1,0:T(8,128)S(1)}) fusion(f32[512,2048]{1,0:T(8,128)} %get-tuple-element.270, f32[512]{0:T(512)S(1)} %get-tuple-element.271, s32[512]{0:T(512)S(1)} %dynamic_slice.43, s32[2048]{0:T(1024)S(1)} %get-tuple-element.303, s32[2048]{0:T(1024)S(1)} %get-tuple-element.302, ...), kind=kOutput, calls=%fused_computation.35.clone.1 | convolution fusion | flops 278920192 | bytes 9070600 | tf_op jit(solution)/shard_map/while/body/eval_jaxpr/dot_general | solution.py:52
  153.8 2.5 fusion.102
  156.3 1.7 fusion.100
  158.0 2.5 fusion.101
  162.1 4.0 %select_reduce_fusion.7 = (f32[512]{0:T(512)S(1)}, f32[512,2048]{1,0:T(8,128)}) fusion(s32[512]{0:T(512)S(1)} %dynamic_slice.43, s32[2048]{0:T(1024)S(1)} %get-tuple-element.303, s32[2048]{0:T(1024)S(1)} %get-tuple-element.302, s32[512]{0:T(512)S(1)} %dynamic_slice.44, bf16[2048,256]{1,0:T(8,128)(2,1)} %get-tuple-element.305, ...), kind=kOutput, calls=%fused_computation.33.clone.1 | convolution fusion | flops 274726400 | bytes 4872196 | tf_op jit(solution)/shard_map/while/body/eval_jaxpr/dot_general | solution.py:52
  166.1 4.7 %fusion.99 = (f32[512]{0:T(512)S(1)}, f32[512]{0:T(512)S(1)}, f32[512,2048]{1,0:T(8,128)S(1)}) fusion(f32[512,2048]{1,0:T(8,128)} %get-tuple-element.270, f32[512]{0:T(512)S(1)} %get-tuple-element.271, s32[512]{0:T(512)S(1)} %dynamic_slice.43, s32[2048]{0:T(1024)S(1)} %get-tuple-element.303, s32[2048]{0:T(1024)S(1)} %get-tuple-element.302, ...), kind=kOutput, calls=%fused_computation.35.clone.1 | convolution fusion | flops 278920192 | bytes 9070600 | tf_op jit(solution)/shard_map/while/body/eval_jaxpr/dot_general | solution.py:52
  170.8 2.5 fusion.102
  173.3 1.7 fusion.100
  175.1 2.5 fusion.101
  179.2 4.0 %select_reduce_fusion.7 = (f32[512]{0:T(512)S(1)}, f32[512,2048]{1,0:T(8,128)}) fusion(s32[512]{0:T(512)S(1)} %dynamic_slice.43, s32[2048]{0:T(1024)S(1)} %get-tuple-element.303, s32[2048]{0:T(1024)S(1)} %get-tuple-element.302, s32[512]{0:T(512)S(1)} %dynamic_slice.44, bf16[2048,256]{1,0:T(8,128)(2,1)} %get-tuple-element.305, ...), kind=kOutput, calls=%fused_computation.33.clone.1 | convolution fusion | flops 274726400 | bytes 4872196 | tf_op jit(solution)/shard_map/while/body/eval_jaxpr/dot_general | solution.py:52
  183.2 4.7 %fusion.99 = (f32[512]{0:T(512)S(1)}, f32[512]{0:T(512)S(1)}, f32[512,2048]{1,0:T(8,128)S(1)}) fusion(f32[512,2048]{1,0:T(8,128)} %get-tuple-element.270, f32[512]{0:T(512)S(1)} %get-tuple-element.271, s32[512]{0:T(512)S(1)} %dynamic_slice.43, s32[2048]{0:T(1024)S(1)} %get-tuple-element.303, s32[2048]{0:T(1024)S(1)} %get-tuple-element.302, ...), kind=kOutput, calls=%fused_computation.35.clone.1 | convolution fusion | flops 278920192 | bytes 9070600 | tf_op jit(solution)/shard_map/while/body/eval_jaxpr/dot_general | solution.py:52
  187.9 2.5 fusion.102
  190.4 1.7 fusion.100
  192.1 2.5 fusion.101
  196.2 4.0 %select_reduce_fusion.7 = (f32[512]{0:T(512)S(1)}, f32[512,2048]{1,0:T(8,128)}) fusion(s32[512]{0:T(512)S(1)} %dynamic_slice.43, s32[2048]{0:T(1024)S(1)} %get-tuple-element.303, s32[2048]{0:T(1024)S(1)} %get-tuple-element.302, s32[512]{0:T(512)S(1)} %dynamic_slice.44, bf16[2048,256]{1,0:T(8,128)(2,1)} %get-tuple-element.305, ...), kind=kOutput, calls=%fused_computation.33.clone.1 | convolution fusion | flops 274726400 | bytes 4872196 | tf_op jit(solution)/shard_map/while/body/eval_jaxpr/dot_general | solution.py:52
  200.2 4.7 %fusion.99 = (f32[512]{0:T(512)S(1)}, f32[512]{0:T(512)S(1)}, f32[512,2048]{1,0:T(8,128)S(1)}) fusion(f32[512,2048]{1,0:T(8,128)} %get-tuple-element.270, f32[512]{0:T(512)S(1)} %get-tuple-element.271, s32[512]{0:T(512)S(1)} %dynamic_slice.43, s32[2048]{0:T(1024)S(1)} %get-tuple-element.303, s32[2048]{0:T(1024)S(1)} %get-tuple-element.302, ...), kind=kOutput, calls=%fused_computation.35.clone.1 | convolution fusion | flops 278920192 | bytes 9070600 | tf_op jit(solution)/shard_map/while/body/eval_jaxpr/dot_general | solution.py:52
  204.9 2.5 fusion.102
  207.4 1.7 fusion.100
  209.1 2.5 fusion.101
  212.1 14.0 %copy.50 = bf16[2,2048,1,256]{3,0,2,1:T(2,128)(2,1)} copy(bf16[2,2048,1,256]{3,1,0,2:T(8,128)(2,1)S(1)} %maximum_bitcast_fusion.2) | data formatting | bytes 4194304 | tf_op jit(solution)/shard_map/reshape | solution.py:108
  226.1 3.7 %all-to-all-start.2 = ((bf16[2,2048,1,256]{3,0,2,1:T(2,128)(2,1)}), bf16[2,2048,1,256]{3,0,2,1:T(2,128)(2,1)S(1)}, u32[]{:S(2)}, u32[]{:S(2)}) async-start(bf16[2,2048,1,256]{3,0,2,1:T(2,128)(2,1)} %copy.50), calls=%async_computation.2 | async-start | bytes 4194304 | tf_op jit(solution)/shard_map/all_to_all | solution.py:109
  229.8 0.7 fusion.70
  231.8 28.2 %all-to-all-done.2 = bf16[2,2048,1,256]{3,0,2,1:T(2,128)(2,1)S(1)} async-done(((bf16[2,2048,1,256]{3,0,2,1:T(2,128)(2,1)}), bf16[2,2048,1,256]{3,0,2,1:T(2,128)(2,1)S(1)}, u32[]{:S(2)}, u32[]{:S(2)}) %all-to-all-start.2) | async-done | bytes 2097184 | tf_op jit(solution)/shard_map/all_to_all | solution.py:109
  260.7 26.8 %collective-permute-done = bf16[2,128,16,256]{3,1,2,0:T(8,128)(2,1)} collective-permute-done((bf16[2,128,16,256]{3,1,2,0:T(8,128)(2,1)S(1)}, bf16[2,128,16,256]{3,1,2,0:T(8,128)(2,1)}, u32[]{:S(2)}, u32[]{:S(2)}) %collective-permute-start) | collective-permute-done | bytes 2097184 | tf_op jit(solution)/shard_map/ppermute | solution.py:18
  287.5 3.0 %copy.55 = bf16[2,128,16,256]{1,3,2,0:T(8,128)(2,1)S(1)} copy(bf16[2,128,16,256]{3,1,2,0:T(8,128)(2,1)} %collective-permute-done) | data formatting | bytes 4194304 | tf_op jit(solution)/shard_map/ppermute | solution.py:18
  290.5 2.7 copy.56
  (80 shorter events, 6.1 us)
Async XLA Ops:
  5.7 39.8 %all-to-all-start = ((bf16[2,128,16,256]{3,1,0,2:T(8,128)(2,1)}), bf16[2,128,16,256]{3,1,0,2:T(8,128)(2,1)S(1)}, u32[]{:S(2)}, u32[]{:S(2)}) async-start(bf16[2,128,16,256]{3,1,0,2:T(8,128)(2,1)} %copy.46), calls=%async_computation | async-start | bytes 4194304 | tf_op jit(solution)/shard_map/all_to_all | solution.py:96
  15.2 36.3 %copy-start.1 = (s32[1,2,4]{2,1,0:T(2,128)S(1)}, s32[1,2,4]{2,1,0:T(2,128)}, u32[]{:S(2)}) copy-start(s32[1,2,4]{2,1,0:T(2,128)} %param.10) | copy-start | bytes 100
  47.1 34.4 %all-to-all-start.1 = ((bf16[2,128,16,256]{3,1,0,2:T(8,128)(2,1)}), bf16[2,128,16,256]{3,1,0,2:T(8,128)(2,1)}, u32[]{:S(2)}, u32[]{:S(2)}) async-start(bf16[2,128,16,256]{3,1,0,2:T(8,128)(2,1)} %bitcast.62), calls=%async_computation.1 | async-start | bytes 4194304 | tf_op jit(solution)/shard_map/all_to_all | solution.py:97
  89.6 4.6 %copy-start.2 = (f32[512,2048]{1,0:T(8,128)S(1)}, f32[512,2048]{1,0:T(8,128)}, u32[]{:S(2)}) copy-start(f32[512,2048]{1,0:T(8,128)} %get-tuple-element.258) | copy-start | bytes 12582916 | tf_op jit(solution)/shard_map/while
  104.4 4.6 %copy-start.2 = (f32[512,2048]{1,0:T(8,128)S(1)}, f32[512,2048]{1,0:T(8,128)}, u32[]{:S(2)}) copy-start(f32[512,2048]{1,0:T(8,128)} %get-tuple-element.258) | copy-start | bytes 12582916 | tf_op jit(solution)/shard_map/while
  119.2 4.6 %copy-start.2 = (f32[512,2048]{1,0:T(8,128)S(1)}, f32[512,2048]{1,0:T(8,128)}, u32[]{:S(2)}) copy-start(f32[512,2048]{1,0:T(8,128)} %get-tuple-element.258) | copy-start | bytes 12582916 | tf_op jit(solution)/shard_map/while
  133.9 4.6 %copy-start.2 = (f32[512,2048]{1,0:T(8,128)S(1)}, f32[512,2048]{1,0:T(8,128)}, u32[]{:S(2)}) copy-start(f32[512,2048]{1,0:T(8,128)} %get-tuple-element.258) | copy-start | bytes 12582916 | tf_op jit(solution)/shard_map/while
  149.1 4.7 %copy-start.3 = (f32[512,2048]{1,0:T(8,128)S(1)}, f32[512,2048]{1,0:T(8,128)}, u32[]{:S(2)}) copy-start(f32[512,2048]{1,0:T(8,128)} %get-tuple-element.270) | copy-start | bytes 12582916 | tf_op jit(solution)/shard_map/while
  166.1 4.7 %copy-start.3 = (f32[512,2048]{1,0:T(8,128)S(1)}, f32[512,2048]{1,0:T(8,128)}, u32[]{:S(2)}) copy-start(f32[512,2048]{1,0:T(8,128)} %get-tuple-element.270) | copy-start | bytes 12582916 | tf_op jit(solution)/shard_map/while
  183.2 4.7 %copy-start.3 = (f32[512,2048]{1,0:T(8,128)S(1)}, f32[512,2048]{1,0:T(8,128)}, u32[]{:S(2)}) copy-start(f32[512,2048]{1,0:T(8,128)} %get-tuple-element.270) | copy-start | bytes 12582916 | tf_op jit(solution)/shard_map/while
  200.2 4.7 %copy-start.3 = (f32[512,2048]{1,0:T(8,128)S(1)}, f32[512,2048]{1,0:T(8,128)}, u32[]{:S(2)}) copy-start(f32[512,2048]{1,0:T(8,128)} %get-tuple-element.270) | copy-start | bytes 12582916 | tf_op jit(solution)/shard_map/while
  212.0 17.7 %copy-start = (s32[1,2]{1,0:T(1,128)S(1)}, s32[1,2]{1,0:T(1,128)}, u32[]{:S(2)}) copy-start(s32[1,2]{1,0:T(1,128)} %param.11) | copy-start | bytes 28
  226.1 33.9 %all-to-all-start.2 = ((bf16[2,2048,1,256]{3,0,2,1:T(2,128)(2,1)}), bf16[2,2048,1,256]{3,0,2,1:T(2,128)(2,1)S(1)}, u32[]{:S(2)}, u32[]{:S(2)}) async-start(bf16[2,2048,1,256]{3,0,2,1:T(2,128)(2,1)} %copy.50), calls=%async_computation.2 | async-start | bytes 4194304 | tf_op jit(solution)/shard_map/all_to_all | solution.py:109
  260.7 26.8 %collective-permute-start = (bf16[2,128,16,256]{3,1,2,0:T(8,128)(2,1)S(1)}, bf16[2,128,16,256]{3,1,2,0:T(8,128)(2,1)}, u32[]{:S(2)}, u32[]{:S(2)}) collective-permute-start(bf16[2,128,16,256]{3,1,2,0:T(8,128)(2,1)S(1)} %pad_maximum_fusion), channel_id=1, source_target_pairs={{112,0},{0,16},{16,32},{32,48},{48,64},{64,80},{80,96},{96,112},{1... | collective-permute-start | bytes 6291464 | tf_op jit(solution)/shard_map/ppermute | solution.py:18
where the time goes:
time: 294 us; the launch traced here: 293 us
  waiting for transfers between devices  113 us (38%)
  matrix products  99.9 us (34%)
  local copies, waits for them, and re-layouts  41.4 us (14%)
  starting transfers between devices  16.2 us (6%)
  other arithmetic  15.1 us (5%)
  loops' own time  6.04 us (2%)
    dot_general x16, matrix products, one_block(): lax.dot_general(query_cols, key_cols, (((1,), (1,)), ((), ())), preferred...  68.2 us
    dot_general x16, matrix products, one_block(): jnp.dot(weights.astype(jnp.bfloat16), value_cols, preferred_element_type=...  31.6 us
    all_to_all x1, waiting for transfers between devices, local(): lax.all_to_all(query_split, 'seq', split_axis=2, concat_axis=1, tiled=True)  30.3 us
    all_to_all x1, waiting for transfers between devices, local(): lax.all_to_all(shortened(contexts), 'seq', split_axis=1, concat_axis=2, t...  28.2 us
    all_to_all x1, waiting for transfers between devices, local(): lax.all_to_all(wide, 'seq', split_axis=2, concat_axis=1, tiled=True)  27.9 us
    ppermute x1, waiting for transfers between devices, passed_along(): return lax.ppermute(block, axis, route)  26.8 us
    reshape x1, local copies, waits for them, and re-layouts, local(): contexts = contexts.reshape(micro, all_rows, 1, per_device * HD)  14 us
    reduce_sum x8, other arithmetic, one_block(): totals = jnp.sum(weights, axis=1, keepdims=True)  13.8 us
  transfers between devices with their start and end apart: 4, of which 4 were waited for; matrix products, arithmetic and copies ran while one was open for 1% of the time, Pallas kernels for 0%

commit v1 on v0

--- a/solution.py
+++ b/solution.py
@@ -6,6 +6,18 @@
 HD = 128
 QH = 32
 KVH = 8
+
+
+def rotated_exchange(x, axis, split, join):
+    ways, here = (lax.axis_size(axis), lax.axis_index(axis))
+    width = x.shape[split] // ways
+    turned = jnp.roll(x, -here * width, axis=split)
+    got = [lax.slice_in_dim(turned, 0, width, axis=split)]
+    for far in range(1, ways):
+        sent = lax.slice_in_dim(turned, far * width, (far + 1) * width, axis=split)
+        got.append(lax.ppermute(sent, axis, [(d, (d + far) % ways) for d in range(ways)]))
+    line = jnp.concatenate(got[::-1], axis=join)
+    return jnp.roll(line, (here + 1) * got[0].shape[join], axis=join)
 
 
 def shortened(value):
@@ -93,7 +105,7 @@
     query_split = queries.reshape(micro, tok_rows, n_seq, per_device * HD)
     wide = jnp.repeat(keys_values.reshape(micro, tok_rows, KVH, 2 * HD), repeat_count, axis=2)
     head_queries, head_pairs = (
-        lax.all_to_all(query_split, "seq", split_axis=2, concat_axis=1, tiled=True),
+        rotated_exchange(query_split, "seq", 2, 1),
         lax.all_to_all(wide, "seq", split_axis=2, concat_axis=1, tiled=True),
     )
     head_queries = head_queries.reshape(micro, all_rows, per_device * HD)

time: 294 us -> 294 us (level)
  starting transfers between devices: 16.2 us -> 45.5 us
  waiting for transfers between devices: 113 us -> 83.8 us
  matrix products: 99.9 us -> 94.3 us
    ppermute x0 -> x15, starting transfers between devices: none -> 35.3 us  [rotated_exchange(): lax.ppermute(sent, axis, [(d, (d + far) % ways) for d in range(ways)])]
    ppermute x0 -> x15, waiting for transfers between devices: none -> 31.2 us  [rotated_exchange(): lax.ppermute(sent, axis, [(d, (d + far) % ways) for d in range(ways)])]
    all_to_all x1 -> x0, waiting for transfers between devices: 30.3 us -> none  [local(): lax.all_to_all(query_split, 'seq', split_axis=2, concat_axis=1, tiled=True)]
    all_to_all x1, waiting for transfers between devices: 27.9 us -> 0.01 us  [local(): lax.all_to_all(wide, 'seq', split_axis=2, concat_axis=1, tiled=True)]
    dot_general x16, matrix products: 31.6 us -> 23.5 us  [one_block(): jnp.dot(weights.astype(jnp.bfloat16), value_cols, preferred_element_type=...]
    all_to_all x1 -> x0, starting transfers between devices: 7.99 us -> none  [local(): lax.all_to_all(query_split, 'seq', split_axis=2, concat_axis=1, tiled=True)]
    unnamed x5 -> x44, local copies, waits for them, and re-layouts: 3.14 us -> 8.87 us
  transfers between devices with their start and end apart: 4 -> 18, of which waited for: 4 -> 7; matrix products, arithmetic and copies ran while one was open for 1% -> 3% of each run, Pallas kernels for 0% -> 0%
where the time goes in v1:
time: 294 us; the launch traced here: 293 us
  matrix products  94.3 us (32%)
  waiting for transfers between devices  83.8 us (29%)
  starting transfers between devices  45.5 us (15%)
  local copies, waits for them, and re-layouts  44.2 us (15%)
  other arithmetic  17.6 us (6%)
  loops' own time  5.72 us (2%)
    dot_general x16, matrix products, one_block(): lax.dot_general(query_cols, key_cols, (((1,), (1,)), ((), ())), preferred...  70.8 us
    ppermute x15, starting transfers between devices, rotated_exchange(): lax.ppermute(sent, axis, [(d, (d + far) % ways) for d in range(ways)])  35.3 us
    ppermute x15, waiting for transfers between devices, rotated_exchange(): lax.ppermute(sent, axis, [(d, (d + far) % ways) for d in range(ways)])  31.2 us
    ppermute x1, waiting for transfers between devices, passed_along(): return lax.ppermute(block, axis, route)  26.8 us
    all_to_all x1, waiting for transfers between devices, local(): lax.all_to_all(shortened(contexts), 'seq', split_axis=1, concat_axis=2, t...  25.8 us
    dot_general x16, matrix products, one_block(): jnp.dot(weights.astype(jnp.bfloat16), value_cols, preferred_element_type=...  23.5 us
    reshape x1, local copies, waits for them, and re-layouts, local(): contexts = contexts.reshape(micro, all_rows, 1, per_device * HD)  14 us
    reduce_sum x8, other arithmetic, one_block(): totals = jnp.sum(weights, axis=1, keepdims=True)  13.8 us
  transfers between devices with their start and end apart: 18, of which 7 were waited for; matrix products, arithmetic and copies ran while one was open for 3% of the time, Pallas kernels for 0%

profile of v1, /device:TPU:0, one launch (start us, length us, event | category | flops | bytes accessed | tf_op | source)
XLA Modules:
  0.0 292.9 jit_solution(15124902686634250611)
XLA Ops:
  0.0 4.1 %copy.39 = bf16[1,2,128,4096]{2,3,1,0:T(8,128)(2,1)} copy(bf16[1,2,128,4096]{3,2,1,0:T(8,128)(2,1)} %param.8) | data formatting | bytes 4194304 | tf_op args[0]
  4.1 2.4 fusion.66
  6.5 1.3 fusion.70
  7.8 6.4 %collective-permute-start = (bf16[2,128,1,256]{1,3,2,0:T(8,128)(2,1)}, bf16[2,128,1,256]{1,3,2,0:T(8,128)(2,1)S(1)}, u32[]{:S(2)}, u32[]{:S(2)}) collective-permute-start(bf16[2,128,1,256]{1,3,2,0:T(8,128)(2,1)} %get-tuple-element.235), channel_id=1, source_target_pairs={{0,15},{1,0},{2,1},{3,2},{4,3},{5,4},{6,5},{7,6},{8,7},{9,8},{10,9... | collective-permute-start | bytes 393224 | tf_op jit(solution)/shard_map/ppermute | solution.py:18
  15.7 1.9 collective-permute-start.4
  17.9 1.6 broadcast_in_dim.48
  19.5 6.5 %all-to-all-start = ((bf16[2,128,16,256]{3,1,0,2:T(8,128)(2,1)}), bf16[2,128,16,256]{3,1,0,2:T(8,128)(2,1)}, u32[]{:S(2)}, u32[]{:S(2)}) async-start(bf16[2,128,16,256]{3,1,0,2:T(8,128)(2,1)} %bitcast.60), calls=%async_computation | async-start | bytes 4194304 | tf_op jit(solution)/shard_map/all_to_all | solution.py:109
  26.6 5.9 %collective-permute-start.5 = (bf16[2,128,1,256]{1,3,2,0:T(8,128)(2,1)S(1)}, bf16[2,128,1,256]{1,3,2,0:T(8,128)(2,1)S(1)}, u32[]{:S(2)}, u32[]{:S(2)}) collective-permute-start(bf16[2,128,1,256]{1,3,2,0:T(8,128)(2,1)S(1)} %copy-done.5), channel_id=1, source_target_pairs={{0,10},{1,11},{2,12},{3,13},{4,14},{5,15},{6,0},{7,1},{8,2},{9,3},... | collective-permute-start | bytes 393224 | tf_op jit(solution)/shard_map/ppermute | solution.py:18
  33.2 3.1 %collective-permute-start.7 = (bf16[2,128,1,256]{1,3,2,0:T(8,128)(2,1)S(1)}, bf16[2,128,1,256]{1,3,2,0:T(8,128)(2,1)S(1)}, u32[]{:S(2)}, u32[]{:S(2)}) collective-permute-start(bf16[2,128,1,256]{1,3,2,0:T(8,128)(2,1)S(1)} %copy-done.3), channel_id=1, source_target_pairs={{0,8},{1,9},{2,10},{3,11},{4,12},{5,13},{6,14},{7,15},{8,0},{9,1},... | collective-permute-start | bytes 393224 | tf_op jit(solution)/shard_map/ppermute | solution.py:18
  37.9 1.8 collective-permute-start.9
  40.6 18.8 %collective-permute-done.5 = bf16[2,128,1,256]{1,3,2,0:T(8,128)(2,1)S(1)} collective-permute-done((bf16[2,128,1,256]{1,3,2,0:T(8,128)(2,1)S(1)}, bf16[2,128,1,256]{1,3,2,0:T(8,128)(2,1)S(1)}, u32[]{:S(2)}, u32[]{:S(2)}) %collective-permute-start.5) | collective-permute-done | bytes 131104 | tf_op jit(solution)/shard_map/ppermute | solution.py:18
  59.9 3.6 %collective-permute-done.6 = bf16[2,128,1,256]{1,3,2,0:T(8,128)(2,1)S(1)} collective-permute-done((bf16[2,128,1,256]{1,3,2,0:T(8,128)(2,1)S(1)}, bf16[2,128,1,256]{1,3,2,0:T(8,128)(2,1)S(1)}, u32[]{:S(2)}, u32[]{:S(2)}) %collective-permute-start.6) | collective-permute-done | bytes 131104 | tf_op jit(solution)/shard_map/ppermute | solution.py:18
  63.6 11.9 %collective-permute-start.12 = (bf16[2,128,1,256]{1,3,2,0:T(8,128)(2,1)}, bf16[2,128,1,256]{1,3,2,0:T(8,128)(2,1)S(1)}, u32[]{:S(2)}, u32[]{:S(2)}) collective-permute-start(bf16[2,128,1,256]{1,3,2,0:T(8,128)(2,1)} %get-tuple-element.223), channel_id=1, source_target_pairs={{0,3},{1,4},{2,5},{3,6},{4,7},{5,8},{6,9},{7,10},{8,11},{9,12},{10... | collective-permute-start | bytes 393224 | tf_op jit(solution)/shard_map/ppermute | solution.py:18
  76.9 2.8 collective-permute-done.12
  79.8 4.7 %collective-permute-done.13 = bf16[2,128,1,256]{1,3,2,0:T(8,128)(2,1)S(1)} collective-permute-done((bf16[2,128,1,256]{1,3,2,0:T(8,128)(2,1)}, bf16[2,128,1,256]{1,3,2,0:T(8,128)(2,1)S(1)}, u32[]{:S(2)}, u32[]{:S(2)}) %collective-permute-start.13) | collective-permute-done | bytes 131104 | tf_op jit(solution)/shard_map/ppermute | solution.py:18
  89.6 3.1 %fusion.69 = (bf16[1,16,128,1,256]{4,2,0,1,3:T(8,128)(2,1)}, bf16[1,16,128,1,256]{4,2,0,1,3:T(8,128)(2,1)}) fusion(bf16[2,16,128,1,256]{4,2,0,1,3:T(8,128)(2,1)} %bitcast.8), kind=kLoop, calls=%fused_computation.109 | loop fusion | bytes 4194304 | tf_op jit(solution)/shard_map/slice | solution.py:115
  92.8 59.5 %while.22 = (s32[]{:T(128)}, bf16[4,512,256]{2,1,0:T(8,128)(2,1)S(1)}, s32[4]{0:T(128)S(1)}, s32[2048]{0:T(1024)S(1)}, s32[2048]{0:T(1024)S(1)}, /*index=5*/bf16...) while((s32[]{:T(128)}, ...), condition=%wide.region_7.8_spmd.clone, body=%wide.region_2.7_spmd.clone.sunk | while | flops 1113323520 | bytes 50462988 | solution.py:84
  94.1 4.2 %select_reduce_fusion.6 = (f32[512]{0:T(512)S(1)}, f32[512,2048]{1,0:T(8,128)}) fusion(s32[512]{0:T(512)S(1)} %dynamic_slice.58, s32[2048]{0:T(1024)S(1)} %get-tuple-element.410, s32[2048]{0:T(1024)S(1)} %get-tuple-element.409, s32[512]{0:T(512)S(1)} %dynamic_slice.59, bf16[2048,256]{1,0:T(8,128)(2,1)} %get-tuple-element.412, ...), kind=kOutput, calls=%fused_computation.3.clone.1 | convolution fusion | flops 274726400 | bytes 4872196 | tf_op jit(solution)/shard_map/while/body/eval_jaxpr/dot_general | solution.py:64
  98.4 4.4 %fusion.92 = (f32[512]{0:T(512)S(1)}, f32[512]{0:T(512)S(1)}, f32[512,2048]{1,0:T(8,128)S(1)}) fusion(f32[512,2048]{1,0:T(8,128)} %get-tuple-element.329, f32[512]{0:T(512)S(1)} %get-tuple-element.330, s32[512]{0:T(512)S(1)} %dynamic_slice.58, s32[2048]{0:T(1024)S(1)} %get-tuple-element.410, s32[2048]{0:T(1024)S(1)} %get-tuple-element.409, ...), kind=kOutput, calls=%fused_computation.5.clone.1 | convolution fusion | flops 278920192 | bytes 9070600 | tf_op jit(solution)/shard_map/while/body/eval_jaxpr/dot_general | solution.py:64
  102.8 1.5 fusion.95
  104.3 1.7 fusion.93
  106.0 1.5 fusion.94
  109.0 4.2 %select_reduce_fusion.6 = (f32[512]{0:T(512)S(1)}, f32[512,2048]{1,0:T(8,128)}) fusion(s32[512]{0:T(512)S(1)} %dynamic_slice.58, s32[2048]{0:T(1024)S(1)} %get-tuple-element.410, s32[2048]{0:T(1024)S(1)} %get-tuple-element.409, s32[512]{0:T(512)S(1)} %dynamic_slice.59, bf16[2048,256]{1,0:T(8,128)(2,1)} %get-tuple-element.412, ...), kind=kOutput, calls=%fused_computation.3.clone.1 | convolution fusion | flops 274726400 | bytes 4872196 | tf_op jit(solution)/shard_map/while/body/eval_jaxpr/dot_general | solution.py:64
  113.2 4.4 %fusion.92 = (f32[512]{0:T(512)S(1)}, f32[512]{0:T(512)S(1)}, f32[512,2048]{1,0:T(8,128)S(1)}) fusion(f32[512,2048]{1,0:T(8,128)} %get-tuple-element.329, f32[512]{0:T(512)S(1)} %get-tuple-element.330, s32[512]{0:T(512)S(1)} %dynamic_slice.58, s32[2048]{0:T(1024)S(1)} %get-tuple-element.410, s32[2048]{0:T(1024)S(1)} %get-tuple-element.409, ...), kind=kOutput, calls=%fused_computation.5.clone.1 | convolution fusion | flops 278920192 | bytes 9070600 | tf_op jit(solution)/shard_map/while/body/eval_jaxpr/dot_general | solution.py:64
  117.7 1.5 fusion.95
  119.2 1.7 fusion.93
  120.9 1.5 fusion.94
  123.9 4.2 %select_reduce_fusion.6 = (f32[512]{0:T(512)S(1)}, f32[512,2048]{1,0:T(8,128)}) fusion(s32[512]{0:T(512)S(1)} %dynamic_slice.58, s32[2048]{0:T(1024)S(1)} %get-tuple-element.410, s32[2048]{0:T(1024)S(1)} %get-tuple-element.409, s32[512]{0:T(512)S(1)} %dynamic_slice.59, bf16[2048,256]{1,0:T(8,128)(2,1)} %get-tuple-element.412, ...), kind=kOutput, calls=%fused_computation.3.clone.1 | convolution fusion | flops 274726400 | bytes 4872196 | tf_op jit(solution)/shard_map/while/body/eval_jaxpr/dot_general | solution.py:64
  128.1 4.4 %fusion.92 = (f32[512]{0:T(512)S(1)}, f32[512]{0:T(512)S(1)}, f32[512,2048]{1,0:T(8,128)S(1)}) fusion(f32[512,2048]{1,0:T(8,128)} %get-tuple-element.329, f32[512]{0:T(512)S(1)} %get-tuple-element.330, s32[512]{0:T(512)S(1)} %dynamic_slice.58, s32[2048]{0:T(1024)S(1)} %get-tuple-element.410, s32[2048]{0:T(1024)S(1)} %get-tuple-element.409, ...), kind=kOutput, calls=%fused_computation.5.clone.1 | convolution fusion | flops 278920192 | bytes 9070600 | tf_op jit(solution)/shard_map/while/body/eval_jaxpr/dot_general | solution.py:64
  132.5 1.5 fusion.95
  134.0 1.7 fusion.93
  135.7 1.5 fusion.94
  138.7 4.2 %select_reduce_fusion.6 = (f32[512]{0:T(512)S(1)}, f32[512,2048]{1,0:T(8,128)}) fusion(s32[512]{0:T(512)S(1)} %dynamic_slice.58, s32[2048]{0:T(1024)S(1)} %get-tuple-element.410, s32[2048]{0:T(1024)S(1)} %get-tuple-element.409, s32[512]{0:T(512)S(1)} %dynamic_slice.59, bf16[2048,256]{1,0:T(8,128)(2,1)} %get-tuple-element.412, ...), kind=kOutput, calls=%fused_computation.3.clone.1 | convolution fusion | flops 274726400 | bytes 4872196 | tf_op jit(solution)/shard_map/while/body/eval_jaxpr/dot_general | solution.py:64
  143.0 4.4 %fusion.92 = (f32[512]{0:T(512)S(1)}, f32[512]{0:T(512)S(1)}, f32[512,2048]{1,0:T(8,128)S(1)}) fusion(f32[512,2048]{1,0:T(8,128)} %get-tuple-element.329, f32[512]{0:T(512)S(1)} %get-tuple-element.330, s32[512]{0:T(512)S(1)} %dynamic_slice.58, s32[2048]{0:T(1024)S(1)} %get-tuple-element.410, s32[2048]{0:T(1024)S(1)} %get-tuple-element.409, ...), kind=kOutput, calls=%fused_computation.5.clone.1 | convolution fusion | flops 278920192 | bytes 9070600 | tf_op jit(solution)/shard_map/while/body/eval_jaxpr/dot_general | solution.py:64
  147.4 1.5 fusion.95
  148.9 1.7 fusion.93
  150.6 1.5 fusion.94
  152.4 61.7 %while.23 = (s32[]{:T(128)}, bf16[4,512,256]{2,1,0:T(8,128)(2,1)S(1)}, s32[4]{0:T(128)S(1)}, s32[2048]{0:T(1024)S(1)}, s32[2048]{0:T(1024)S(1)}, /*index=5*/bf16...) while((s32[]{:T(128)}, ...), condition=%wide.region_15.16_spmd.clone, body=%wide.region_10.15_spmd.clone.sunk | while | flops 1113323520 | bytes 50462988 | solution.py:84
  154.0 4.3 %select_reduce_fusion.7 = (f32[512]{0:T(512)S(1)}, f32[512,2048]{1,0:T(8,128)}) fusion(s32[512]{0:T(512)S(1)} %dynamic_slice.61, s32[2048]{0:T(1024)S(1)} %get-tuple-element.374, s32[2048]{0:T(1024)S(1)} %get-tuple-element.373, s32[512]{0:T(512)S(1)} %dynamic_slice.62, bf16[2048,256]{1,0:T(8,128)(2,1)} %get-tuple-element.376, ...), kind=kOutput, calls=%fused_computation.33.clone.1 | convolution fusion | flops 274726400 | bytes 4872196 | tf_op jit(solution)/shard_map/while/body/eval_jaxpr/dot_general | solution.py:64
  158.3 4.8 %fusion.100 = (f32[512]{0:T(512)S(1)}, f32[512]{0:T(512)S(1)}, f32[512,2048]{1,0:T(8,128)S(1)}) fusion(f32[512,2048]{1,0:T(8,128)} %get-tuple-element.341, f32[512]{0:T(512)S(1)} %get-tuple-element.342, s32[512]{0:T(512)S(1)} %dynamic_slice.61, s32[2048]{0:T(1024)S(1)} %get-tuple-element.374, s32[2048]{0:T(1024)S(1)} %get-tuple-element.373, ...), kind=kOutput, calls=%fused_computation.35.clone.1 | convolution fusion | flops 278920192 | bytes 9070600 | tf_op jit(solution)/shard_map/while/body/eval_jaxpr/dot_general | solution.py:64
  163.1 1.5 fusion.103
  164.6 1.7 fusion.101
  166.3 1.5 fusion.102
  169.4 4.3 %select_reduce_fusion.7 = (f32[512]{0:T(512)S(1)}, f32[512,2048]{1,0:T(8,128)}) fusion(s32[512]{0:T(512)S(1)} %dynamic_slice.61, s32[2048]{0:T(1024)S(1)} %get-tuple-element.374, s32[2048]{0:T(1024)S(1)} %get-tuple-element.373, s32[512]{0:T(512)S(1)} %dynamic_slice.62, bf16[2048,256]{1,0:T(8,128)(2,1)} %get-tuple-element.376, ...), kind=kOutput, calls=%fused_computation.33.clone.1 | convolution fusion | flops 274726400 | bytes 4872196 | tf_op jit(solution)/shard_map/while/body/eval_jaxpr/dot_general | solution.py:64
  173.7 4.8 %fusion.100 = (f32[512]{0:T(512)S(1)}, f32[512]{0:T(512)S(1)}, f32[512,2048]{1,0:T(8,128)S(1)}) fusion(f32[512,2048]{1,0:T(8,128)} %get-tuple-element.341, f32[512]{0:T(512)S(1)} %get-tuple-element.342, s32[512]{0:T(512)S(1)} %dynamic_slice.61, s32[2048]{0:T(1024)S(1)} %get-tuple-element.374, s32[2048]{0:T(1024)S(1)} %get-tuple-element.373, ...), kind=kOutput, calls=%fused_computation.35.clone.1 | convolution fusion | flops 278920192 | bytes 9070600 | tf_op jit(solution)/shard_map/while/body/eval_jaxpr/dot_general | solution.py:64
  178.5 1.5 fusion.103
  180.0 1.7 fusion.101
  181.7 1.5 fusion.102
  184.8 4.3 %select_reduce_fusion.7 = (f32[512]{0:T(512)S(1)}, f32[512,2048]{1,0:T(8,128)}) fusion(s32[512]{0:T(512)S(1)} %dynamic_slice.61, s32[2048]{0:T(1024)S(1)} %get-tuple-element.374, s32[2048]{0:T(1024)S(1)} %get-tuple-element.373, s32[512]{0:T(512)S(1)} %dynamic_slice.62, bf16[2048,256]{1,0:T(8,128)(2,1)} %get-tuple-element.376, ...), kind=kOutput, calls=%fused_computation.33.clone.1 | convolution fusion | flops 274726400 | bytes 4872196 | tf_op jit(solution)/shard_map/while/body/eval_jaxpr/dot_general | solution.py:64
  189.1 4.8 %fusion.100 = (f32[512]{0:T(512)S(1)}, f32[512]{0:T(512)S(1)}, f32[512,2048]{1,0:T(8,128)S(1)}) fusion(f32[512,2048]{1,0:T(8,128)} %get-tuple-element.341, f32[512]{0:T(512)S(1)} %get-tuple-element.342, s32[512]{0:T(512)S(1)} %dynamic_slice.61, s32[2048]{0:T(1024)S(1)} %get-tuple-element.374, s32[2048]{0:T(1024)S(1)} %get-tuple-element.373, ...), kind=kOutput, calls=%fused_computation.35.clone.1 | convolution fusion | flops 278920192 | bytes 9070600 | tf_op jit(solution)/shard_map/while/body/eval_jaxpr/dot_general | solution.py:64
  193.9 1.5 fusion.103
  195.3 1.7 fusion.101
  197.1 1.5 fusion.102
  200.1 4.3 %select_reduce_fusion.7 = (f32[512]{0:T(512)S(1)}, f32[512,2048]{1,0:T(8,128)}) fusion(s32[512]{0:T(512)S(1)} %dynamic_slice.61, s32[2048]{0:T(1024)S(1)} %get-tuple-element.374, s32[2048]{0:T(1024)S(1)} %get-tuple-element.373, s32[512]{0:T(512)S(1)} %dynamic_slice.62, bf16[2048,256]{1,0:T(8,128)(2,1)} %get-tuple-element.376, ...), kind=kOutput, calls=%fused_computation.33.clone.1 | convolution fusion | flops 274726400 | bytes 4872196 | tf_op jit(solution)/shard_map/while/body/eval_jaxpr/dot_general | solution.py:64
  204.4 4.8 %fusion.100 = (f32[512]{0:T(512)S(1)}, f32[512]{0:T(512)S(1)}, f32[512,2048]{1,0:T(8,128)S(1)}) fusion(f32[512,2048]{1,0:T(8,128)} %get-tuple-element.341, f32[512]{0:T(512)S(1)} %get-tuple-element.342, s32[512]{0:T(512)S(1)} %dynamic_slice.61, s32[2048]{0:T(1024)S(1)} %get-tuple-element.374, s32[2048]{0:T(1024)S(1)} %get-tuple-element.373, ...), kind=kOutput, calls=%fused_computation.35.clone.1 | convolution fusion | flops 278920192 | bytes 9070600 | tf_op jit(solution)/shard_map/while/body/eval_jaxpr/dot_general | solution.py:64
  209.2 1.5 fusion.103
  210.7 1.7 fusion.101
  212.4 1.5 fusion.102
  214.3 14.0 %copy.45 = bf16[2,2048,1,256]{3,0,2,1:T(2,128)(2,1)} copy(bf16[2,2048,1,256]{3,1,0,2:T(8,128)(2,1)S(1)} %maximum_bitcast_fusion.2) | data formatting | bytes 4194304 | tf_op jit(solution)/shard_map/reshape | solution.py:120
  228.3 3.7 %all-to-all-start.1 = ((bf16[2,2048,1,256]{3,0,2,1:T(2,128)(2,1)}), bf16[2,2048,1,256]{3,0,2,1:T(2,128)(2,1)S(1)}, u32[]{:S(2)}, u32[]{:S(2)}) async-start(bf16[2,2048,1,256]{3,0,2,1:T(2,128)(2,1)} %copy.45), calls=%async_computation.1 | async-start | bytes 4194304 | tf_op jit(solution)/shard_map/all_to_all | solution.py:121
  233.8 25.8 %all-to-all-done.1 = bf16[2,2048,1,256]{3,0,2,1:T(2,128)(2,1)S(1)} async-done(((bf16[2,2048,1,256]{3,0,2,1:T(2,128)(2,1)}), bf16[2,2048,1,256]{3,0,2,1:T(2,128)(2,1)S(1)}, u32[]{:S(2)}, u32[]{:S(2)}) %all-to-all-start.1) | async-done | bytes 2097184 | tf_op jit(solution)/shard_map/all_to_all | solution.py:121
  260.3 26.8 %collective-permute-done.15 = bf16[2,128,16,256]{3,1,2,0:T(8,128)(2,1)} collective-permute-done((bf16[2,128,16,256]{3,1,2,0:T(8,128)(2,1)S(1)}, bf16[2,128,16,256]{3,1,2,0:T(8,128)(2,1)}, u32[]{:S(2)}, u32[]{:S(2)}) %collective-permute-start.15) | collective-permute-done | bytes 2097184 | tf_op jit(solution)/shard_map/ppermute | solution.py:30
  287.1 3.0 %copy.50 = bf16[2,128,16,256]{1,3,2,0:T(8,128)(2,1)S(1)} copy(bf16[2,128,16,256]{3,1,2,0:T(8,128)(2,1)} %collective-permute-done.15) | data formatting | bytes 4194304 | tf_op jit(solution)/shard_map/ppermute | solution.py:30
  290.1 2.7 copy.51
  (165 shorter events, 21.5 us)
Async XLA Ops:
  4.1 13.6 %copy-start = (bf16[1,2,128,8,256]{4,3,2,1,0:T(8,128)(2,1)S(1)}, bf16[1,2,128,8,256]{4,3,2,1,0:T(8,128)(2,1)}, u32[]{:S(2)}) copy-start(bf16[1,2,128,8,256]{4,3,2,1,0:T(8,128)(2,1)} %param.9) | copy-start | bytes 3145732
  7.8 18.8 %collective-permute-start = (bf16[2,128,1,256]{1,3,2,0:T(8,128)(2,1)}, bf16[2,128,1,256]{1,3,2,0:T(8,128)(2,1)S(1)}, u32[]{:S(2)}, u32[]{:S(2)}) collective-permute-start(bf16[2,128,1,256]{1,3,2,0:T(8,128)(2,1)} %get-tuple-element.235), channel_id=1, source_target_pairs={{0,15},{1,0},{2,1},{3,2},{4,3},{5,4},{6,5},{7,6},{8,7},{9,8},{10,9... | collective-permute-start | bytes 393224 | tf_op jit(solution)/shard_map/ppermute | solution.py:18
  14.2 18.3 %collective-permute-start.1 = (bf16[2,128,1,256]{1,3,2,0:T(8,128)(2,1)}, bf16[2,128,1,256]{1,3,2,0:T(8,128)(2,1)S(1)}, u32[]{:S(2)}, u32[]{:S(2)}) collective-permute-start(bf16[2,128,1,256]{1,3,2,0:T(8,128)(2,1)} %get-tuple-element.234), channel_id=1, source_target_pairs={{0,14},{1,15},{2,0},{3,1},{4,2},{5,3},{6,4},{7,5},{8,6},{9,7},{10,... | collective-permute-start | bytes 393224 | tf_op jit(solution)/shard_map/ppermute | solution.py:18
  14.9 18.2 %collective-permute-start.2 = (bf16[2,128,1,256]{1,3,2,0:T(8,128)(2,1)}, bf16[2,128,1,256]{1,3,2,0:T(8,128)(2,1)S(1)}, u32[]{:S(2)}, u32[]{:S(2)}) collective-permute-start(bf16[2,128,1,256]{1,3,2,0:T(8,128)(2,1)} %get-tuple-element.233), channel_id=1, source_target_pairs={{0,13},{1,14},{2,15},{3,0},{4,1},{5,2},{6,3},{7,4},{8,5},{9,6},{10... | collective-permute-start | bytes 393224 | tf_op jit(solution)/shard_map/ppermute | solution.py:18
  15.6 20.6 %collective-permute-start.3 = (bf16[2,128,1,256]{1,3,2,0:T(8,128)(2,1)}, bf16[2,128,1,256]{1,3,2,0:T(8,128)(2,1)}, u32[]{:S(2)}, u32[]{:S(2)}) collective-permute-start(bf16[2,128,1,256]{1,3,2,0:T(8,128)(2,1)} %get-tuple-element.232), channel_id=1, source_target_pairs={{0,12},{1,13},{2,14},{3,15},{4,0},{5,1},{6,2},{7,3},{8,4},{9,5},{1... | collective-permute-start | bytes 393224 | tf_op jit(solution)/shard_map/ppermute | solution.py:18
  15.7 22.2 %collective-permute-start.4 = (bf16[2,128,1,256]{1,3,2,0:T(8,128)(2,1)}, bf16[2,128,1,256]{1,3,2,0:T(8,128)(2,1)}, u32[]{:S(2)}, u32[]{:S(2)}) collective-permute-start(bf16[2,128,1,256]{1,3,2,0:T(8,128)(2,1)} %get-tuple-element.231), channel_id=1, source_target_pairs={{0,11},{1,12},{2,13},{3,14},{4,15},{5,0},{6,1},{7,2},{8,3},{9,4},{... | collective-permute-start | bytes 393224 | tf_op jit(solution)/shard_map/ppermute | solution.py:18
  17.9 8.1 %copy-start.7 = (s32[1,2,4]{2,1,0:T(2,128)S(1)}, s32[1,2,4]{2,1,0:T(2,128)}, u32[]{:S(2)}) copy-start(s32[1,2,4]{2,1,0:T(2,128)} %param.10) | copy-start | bytes 100
  17.9 8.7 %copy-start.5 = (bf16[2,128,1,256]{1,3,2,0:T(8,128)(2,1)S(1)}, bf16[2,128,1,256]{1,3,2,0:T(8,128)(2,1)}, u32[]{:S(2)}) copy-start(bf16[2,128,1,256]{1,3,2,0:T(8,128)(2,1)} %get-tuple-element.230) | copy-start | bytes 393220
  17.9 14.6 %copy-start.4 = (bf16[2,128,1,256]{1,3,2,0:T(8,128)(2,1)S(1)}, bf16[2,128,1,256]{1,3,2,0:T(8,128)(2,1)}, u32[]{:S(2)}) copy-start(bf16[2,128,1,256]{1,3,2,0:T(8,128)(2,1)} %get-tuple-element.229) | copy-start | bytes 393220
  17.9 15.3 %copy-start.3 = (bf16[2,128,1,256]{1,3,2,0:T(8,128)(2,1)S(1)}, bf16[2,128,1,256]{1,3,2,0:T(8,128)(2,1)}, u32[]{:S(2)}) copy-start(bf16[2,128,1,256]{1,3,2,0:T(8,128)(2,1)} %get-tuple-element.228) | copy-start | bytes 393220
  19.5 70.2 %all-to-all-start = ((bf16[2,128,16,256]{3,1,0,2:T(8,128)(2,1)}), bf16[2,128,16,256]{3,1,0,2:T(8,128)(2,1)}, u32[]{:S(2)}, u32[]{:S(2)}) async-start(bf16[2,128,16,256]{3,1,0,2:T(8,128)(2,1)} %bitcast.60), calls=%async_computation | async-start | bytes 4194304 | tf_op jit(solution)/shard_map/all_to_all | solution.py:109
  26.6 32.8 %collective-permute-start.5 = (bf16[2,128,1,256]{1,3,2,0:T(8,128)(2,1)S(1)}, bf16[2,128,1,256]{1,3,2,0:T(8,128)(2,1)S(1)}, u32[]{:S(2)}, u32[]{:S(2)}) collective-permute-start(bf16[2,128,1,256]{1,3,2,0:T(8,128)(2,1)S(1)} %copy-done.5), channel_id=1, source_target_pairs={{0,10},{1,11},{2,12},{3,13},{4,14},{5,15},{6,0},{7,1},{8,2},{9,3},... | collective-permute-start | bytes 393224 | tf_op jit(solution)/shard_map/ppermute | solution.py:18
  32.5 31.0 %collective-permute-start.6 = (bf16[2,128,1,256]{1,3,2,0:T(8,128)(2,1)S(1)}, bf16[2,128,1,256]{1,3,2,0:T(8,128)(2,1)S(1)}, u32[]{:S(2)}, u32[]{:S(2)}) collective-permute-start(bf16[2,128,1,256]{1,3,2,0:T(8,128)(2,1)S(1)} %copy-done.4), channel_id=1, source_target_pairs={{0,9},{1,10},{2,11},{3,12},{4,13},{5,14},{6,15},{7,0},{8,1},{9,2},... | collective-permute-start | bytes 393224 | tf_op jit(solution)/shard_map/ppermute | solution.py:18
  33.2 30.4 %collective-permute-start.7 = (bf16[2,128,1,256]{1,3,2,0:T(8,128)(2,1)S(1)}, bf16[2,128,1,256]{1,3,2,0:T(8,128)(2,1)S(1)}, u32[]{:S(2)}, u32[]{:S(2)}) collective-permute-start(bf16[2,128,1,256]{1,3,2,0:T(8,128)(2,1)S(1)} %copy-done.3), channel_id=1, source_target_pairs={{0,8},{1,9},{2,10},{3,11},{4,12},{5,13},{6,14},{7,15},{8,0},{9,1},... | collective-permute-start | bytes 393224 | tf_op jit(solution)/shard_map/ppermute | solution.py:18
  36.3 39.2 %collective-permute-start.8 = (bf16[2,128,1,256]{1,3,2,0:T(8,128)(2,1)}, bf16[2,128,1,256]{1,3,2,0:T(8,128)(2,1)S(1)}, u32[]{:S(2)}, u32[]{:S(2)}) collective-permute-start(bf16[2,128,1,256]{1,3,2,0:T(8,128)(2,1)} %get-tuple-element.227), channel_id=1, source_target_pairs={{0,7},{1,8},{2,9},{3,10},{4,11},{5,12},{6,13},{7,14},{8,15},{9,0},... | collective-permute-start | bytes 393224 | tf_op jit(solution)/shard_map/ppermute | solution.py:18
  37.9 37.7 %collective-permute-start.9 = (bf16[2,128,1,256]{1,3,2,0:T(8,128)(2,1)}, bf16[2,128,1,256]{1,3,2,0:T(8,128)(2,1)S(1)}, u32[]{:S(2)}, u32[]{:S(2)}) collective-permute-start(bf16[2,128,1,256]{1,3,2,0:T(8,128)(2,1)} %get-tuple-element.226), channel_id=1, source_target_pairs={{0,6},{1,7},{2,8},{3,9},{4,10},{5,11},{6,12},{7,13},{8,14},{9,15},... | collective-permute-start | bytes 393224 | tf_op jit(solution)/shard_map/ppermute | solution.py:18
  59.4 17.4 %collective-permute-start.10 = (bf16[2,128,1,256]{1,3,2,0:T(8,128)(2,1)}, bf16[2,128,1,256]{1,3,2,0:T(8,128)(2,1)S(1)}, u32[]{:S(2)}, u32[]{:S(2)}) collective-permute-start(bf16[2,128,1,256]{1,3,2,0:T(8,128)(2,1)} %get-tuple-element.225), channel_id=1, source_target_pairs={{0,5},{1,6},{2,7},{3,8},{4,9},{5,10},{6,11},{7,12},{8,13},{9,14},{... | collective-permute-start | bytes 393224 | tf_op jit(solution)/shard_map/ppermute | solution.py:18
  63.5 13.4 %collective-permute-start.11 = (bf16[2,128,1,256]{1,3,2,0:T(8,128)(2,1)}, bf16[2,128,1,256]{1,3,2,0:T(8,128)(2,1)S(1)}, u32[]{:S(2)}, u32[]{:S(2)}) collective-permute-start(bf16[2,128,1,256]{1,3,2,0:T(8,128)(2,1)} %get-tuple-element.224), channel_id=1, source_target_pairs={{0,4},{1,5},{2,6},{3,7},{4,8},{5,9},{6,10},{7,11},{8,12},{9,13},{1... | collective-permute-start | bytes 393224 | tf_op jit(solution)/shard_map/ppermute | solution.py:18
  63.6 16.2 %collective-permute-start.12 = (bf16[2,128,1,256]{1,3,2,0:T(8,128)(2,1)}, bf16[2,128,1,256]{1,3,2,0:T(8,128)(2,1)S(1)}, u32[]{:S(2)}, u32[]{:S(2)}) collective-permute-start(bf16[2,128,1,256]{1,3,2,0:T(8,128)(2,1)} %get-tuple-element.223), channel_id=1, source_target_pairs={{0,3},{1,4},{2,5},{3,6},{4,7},{5,8},{6,9},{7,10},{8,11},{9,12},{10... | collective-permute-start | bytes 393224 | tf_op jit(solution)/shard_map/ppermute | solution.py:18
  75.5 9.0 %collective-permute-start.13 = (bf16[2,128,1,256]{1,3,2,0:T(8,128)(2,1)}, bf16[2,128,1,256]{1,3,2,0:T(8,128)(2,1)S(1)}, u32[]{:S(2)}, u32[]{:S(2)}) collective-permute-start(bf16[2,128,1,256]{1,3,2,0:T(8,128)(2,1)} %get-tuple-element.222), channel_id=1, source_target_pairs={{0,2},{1,3},{2,4},{3,5},{4,6},{5,7},{6,8},{7,9},{8,10},{9,11},{10,... | collective-permute-start | bytes 393224 | tf_op jit(solution)/shard_map/ppermute | solution.py:18
  75.7 10.1 %collective-permute-start.14 = (bf16[2,128,1,256]{1,3,2,0:T(8,128)(2,1)}, bf16[2,128,1,256]{1,3,2,0:T(8,128)(2,1)S(1)}, u32[]{:S(2)}, u32[]{:S(2)}) collective-permute-start(bf16[2,128,1,256]{1,3,2,0:T(8,128)(2,1)} %get-tuple-element.221), channel_id=1, source_target_pairs={{0,1},{1,2},{2,3},{3,4},{4,5},{5,6},{6,7},{7,8},{8,9},{9,10},{10,1... | collective-permute-start | bytes 393224 | tf_op jit(solution)/shard_map/ppermute | solution.py:18
  98.4 4.4 %copy-start.2 = (bf16[2048,256]{1,0:T(8,128)(2,1)S(1)}, bf16[2048,256]{1,0:T(8,128)(2,1)}, u32[]{:S(2)}) copy-start(bf16[2048,256]{1,0:T(8,128)(2,1)} %get-tuple-element.412) | copy-start | bytes 3145732 | tf_op jit(solution)/shard_map/while
  98.4 4.4 %copy-start.8 = (f32[512,2048]{1,0:T(8,128)S(1)}, f32[512,2048]{1,0:T(8,128)}, u32[]{:S(2)}) copy-start(f32[512,2048]{1,0:T(8,128)} %get-tuple-element.329) | copy-start | bytes 12582916 | tf_op jit(solution)/shard_map/while
  113.2 4.4 %copy-start.2 = (bf16[2048,256]{1,0:T(8,128)(2,1)S(1)}, bf16[2048,256]{1,0:T(8,128)(2,1)}, u32[]{:S(2)}) copy-start(bf16[2048,256]{1,0:T(8,128)(2,1)} %get-tuple-element.412) | copy-start | bytes 3145732 | tf_op jit(solution)/shard_map/while
  113.2 4.4 %copy-start.8 = (f32[512,2048]{1,0:T(8,128)S(1)}, f32[512,2048]{1,0:T(8,128)}, u32[]{:S(2)}) copy-start(f32[512,2048]{1,0:T(8,128)} %get-tuple-element.329) | copy-start | bytes 12582916 | tf_op jit(solution)/shard_map/while
  128.1 4.4 %copy-start.2 = (bf16[2048,256]{1,0:T(8,128)(2,1)S(1)}, bf16[2048,256]{1,0:T(8,128)(2,1)}, u32[]{:S(2)}) copy-start(bf16[2048,256]{1,0:T(8,128)(2,1)} %get-tuple-element.412) | copy-start | bytes 3145732 | tf_op jit(solution)/shard_map/while
  128.1 4.4 %copy-start.8 = (f32[512,2048]{1,0:T(8,128)S(1)}, f32[512,2048]{1,0:T(8,128)}, u32[]{:S(2)}) copy-start(f32[512,2048]{1,0:T(8,128)} %get-tuple-element.329) | copy-start | bytes 12582916 | tf_op jit(solution)/shard_map/while
  143.0 4.4 %copy-start.2 = (bf16[2048,256]{1,0:T(8,128)(2,1)S(1)}, bf16[2048,256]{1,0:T(8,128)(2,1)}, u32[]{:S(2)}) copy-start(bf16[2048,256]{1,0:T(8,128)(2,1)} %get-tuple-element.412) | copy-start | bytes 3145732 | tf_op jit(solution)/shard_map/while
  143.0 4.4 %copy-start.8 = (f32[512,2048]{1,0:T(8,128)S(1)}, f32[512,2048]{1,0:T(8,128)}, u32[]{:S(2)}) copy-start(f32[512,2048]{1,0:T(8,128)} %get-tuple-element.329) | copy-start | bytes 12582916 | tf_op jit(solution)/shard_map/while
  152.6 5.7 %copy-start.1 = (bf16[2048,256]{1,0:T(8,128)(2,1)S(1)}, bf16[2048,256]{1,0:T(8,128)(2,1)}, u32[]{:S(2)}) copy-start(bf16[2048,256]{1,0:T(8,128)(2,1)} %get-tuple-element.376) | copy-start | bytes 3145732 | tf_op jit(solution)/shard_map/while
  158.3 4.8 %copy-start.9 = (f32[512,2048]{1,0:T(8,128)S(1)}, f32[512,2048]{1,0:T(8,128)}, u32[]{:S(2)}) copy-start(f32[512,2048]{1,0:T(8,128)} %get-tuple-element.341) | copy-start | bytes 12582916 | tf_op jit(solution)/shard_map/while
  168.0 5.7 %copy-start.1 = (bf16[2048,256]{1,0:T(8,128)(2,1)S(1)}, bf16[2048,256]{1,0:T(8,128)(2,1)}, u32[]{:S(2)}) copy-start(bf16[2048,256]{1,0:T(8,128)(2,1)} %get-tuple-element.376) | copy-start | bytes 3145732 | tf_op jit(solution)/shard_map/while
  173.7 4.8 %copy-start.9 = (f32[512,2048]{1,0:T(8,128)S(1)}, f32[512,2048]{1,0:T(8,128)}, u32[]{:S(2)}) copy-start(f32[512,2048]{1,0:T(8,128)} %get-tuple-element.341) | copy-start | bytes 12582916 | tf_op jit(solution)/shard_map/while
  183.4 5.7 %copy-start.1 = (bf16[2048,256]{1,0:T(8,128)(2,1)S(1)}, bf16[2048,256]{1,0:T(8,128)(2,1)}, u32[]{:S(2)}) copy-start(bf16[2048,256]{1,0:T(8,128)(2,1)} %get-tuple-element.376) | copy-start | bytes 3145732 | tf_op jit(solution)/shard_map/while
  189.1 4.8 %copy-start.9 = (f32[512,2048]{1,0:T(8,128)S(1)}, f32[512,2048]{1,0:T(8,128)}, u32[]{:S(2)}) copy-start(f32[512,2048]{1,0:T(8,128)} %get-tuple-element.341) | copy-start | bytes 12582916 | tf_op jit(solution)/shard_map/while
  198.7 5.7 %copy-start.1 = (bf16[2048,256]{1,0:T(8,128)(2,1)S(1)}, bf16[2048,256]{1,0:T(8,128)(2,1)}, u32[]{:S(2)}) copy-start(bf16[2048,256]{1,0:T(8,128)(2,1)} %get-tuple-element.376) | copy-start | bytes 3145732 | tf_op jit(solution)/shard_map/while
  204.4 4.8 %copy-start.9 = (f32[512,2048]{1,0:T(8,128)S(1)}, f32[512,2048]{1,0:T(8,128)}, u32[]{:S(2)}) copy-start(f32[512,2048]{1,0:T(8,128)} %get-tuple-element.341) | copy-start | bytes 12582916 | tf_op jit(solution)/shard_map/while
  214.3 17.7 %copy-start.6 = (s32[1,2]{1,0:T(1,128)S(1)}, s32[1,2]{1,0:T(1,128)}, u32[]{:S(2)}) copy-start(s32[1,2]{1,0:T(1,128)} %param.11) | copy-start | bytes 28
  228.3 31.3 %all-to-all-start.1 = ((bf16[2,2048,1,256]{3,0,2,1:T(2,128)(2,1)}), bf16[2,2048,1,256]{3,0,2,1:T(2,128)(2,1)S(1)}, u32[]{:S(2)}, u32[]{:S(2)}) async-start(bf16[2,2048,1,256]{3,0,2,1:T(2,128)(2,1)} %copy.45), calls=%async_computation.1 | async-start | bytes 4194304 | tf_op jit(solution)/shard_map/all_to_all | solution.py:121
  260.3 26.8 %collective-permute-start.15 = (bf16[2,128,16,256]{3,1,2,0:T(8,128)(2,1)S(1)}, bf16[2,128,16,256]{3,1,2,0:T(8,128)(2,1)}, u32[]{:S(2)}, u32[]{:S(2)}) collective-permute-start(bf16[2,128,16,256]{3,1,2,0:T(8,128)(2,1)S(1)} %pad_maximum_fusion), channel_id=1, source_target_pairs={{112,0},{0,16},{16,32},{32,48},{48,64},{64,80},{80,96},{96,112},{1... | collective-permute-start | bytes 6291464 | tf_op jit(solution)/shard_map/ppermute | solution.py:30
